TPU v7x, 512 devices: a whole 4x8x8 slice. The times are simulated.
512 devices in a mesh: region: 32 (over x, z), tm: 16 (over y, core).
Axes of the slice: x: 4, y: 8, z: 8, core: 2. Of those that a mesh axis runs over, the one named last changes fastest.
Arguments:
- right_side: float32 [1024, 65536], P('tm', 'region'), may hold values from -9 to 9
- initial: float32 [1024, 65536], P('tm', 'region'), may hold values from -1.5 to 1.5
- blocks: bfloat16 [512, 9, 128, 128], P(('region', 'tm')), may hold values from -2.5 to 3.1, as said below
- neighbour_blocks: int32 [512, 8], P('region'), may hold values from 0 to 511, as said below
- temporal_cov: bfloat16 [1024, 1024], P('tm'), may hold values from -2.5 to 2.8, as said below
Outputs:
- solution: float32 [1024, 65536], P('tm', 'region')
- residual: float32 [1024, 65536], P('tm', 'region')
Inputs may be any that keep to these rules, and one draw needn't show every extreme that they name: blocks[i, 0] is symmetric positive definite. `neighbour_blocks`: each column names every block exactly once. Blocks fall into cyclic windows of 16 consecutive blocks starting at 8 + m * 16, and every block listed for row i lies in the window of i. temporal_cov is symmetric positive definite.
All inputs are finite; a program needn't handle non-finite values.
Results may differ from a plain program's by a relative error of at most 0.012.
The roundings to bfloat16 on the way count: a program that leaves them out, or rounds other values in their place, can miss the bound.
Values may be sent and summed in bfloat16 or wider, within the bound.
No kernel may reach another device: no remote copies, remote signals or barrier semaphores. Data moves between devices by JAX's collectives and lax.ppermute only.
A program may use at most 64 MiB of HBM per device.

v0:
```python
import jax
import jax.numpy as jnp
from jax import lax
from jax.sharding import Mesh
from jax.sharding import PartitionSpec as P

ITERS = 2
REGION = ("region_0", "region_1")
TM = ("tm_0", "tm_1")
REGION_TM = ("region_0", "region_1", "tm_0", "tm_1")


def with_halo(value, sides, width):
    for axis, dim in sides:
        peers, length = (lax.axis_size(axis), value.shape[dim])
        up = [(i, (i + 1) % peers) for i in range(peers)]
        down = [(j, i) for i, j in up]
        last = lax.slice_in_dim(value, length - width, length, axis=dim)
        initial = lax.slice_in_dim(value, 0, width, axis=dim)
        before = lax.ppermute(last, axis, up)
        after = lax.ppermute(initial, axis, down)
        value = jnp.concatenate([before, value, after], axis=dim)
    return value


def gather_axes(value, axes, dim):
    for axis in reversed(axes):
        value = lax.all_gather(value, axis, axis=dim, tiled=True)
    return value


def one_axis_at_a_time(value, axes):
    for axis in axes:
        value = lax.psum(value, axis)
    return value


def local_tiles(lowered, neighbour_blocks):
    row_count = neighbour_blocks.shape[0]
    tile_width = lowered.shape[1] // row_count
    widened = with_halo(lowered, ((REGION, 1),), row_count // 2 * tile_width)
    region = lax.axis_index(REGION)
    block_total = row_count * lax.axis_size(REGION)
    offset = jnp.mod(neighbour_blocks - region * row_count + row_count // 2, block_total)
    itself = (jnp.arange(row_count, dtype=jnp.int32) + row_count // 2)[:, None]
    places = jnp.concatenate([itself, offset], axis=1)
    cell_tiles = widened.reshape(widened.shape[0], 2 * row_count, tile_width)
    return jnp.take(cell_tiles, places, axis=1)


def local(right_side, initial, blocks, neighbour_blocks, temporal_cov):
    hour_matrix = gather_axes(temporal_cov, TM, 0)
    region_blocks = lax.all_gather(blocks, TM, axis=0, tiled=True)
    tm_count = lax.axis_size(TM)
    hour_slice = right_side.shape[0]
    site_count = right_side.shape[1]
    tile_width = blocks.shape[2]
    own_rows = blocks.shape[0]

    def temporal(arrived):
        item_count = arrived.shape[2]
        flattened = arrived.reshape(arrived.shape[0], item_count * tile_width)
        blended = jnp.dot(hour_matrix, flattened, preferred_element_type=jnp.float32).astype(
            jnp.bfloat16
        )
        return blended.reshape(arrived.shape[0], 1, item_count, tile_width)

    def operate(current):
        lowered = current.astype(jnp.bfloat16)
        tile_stack = local_tiles(lowered, neighbour_blocks)
        spatial = jnp.einsum(
            "hrkb,rkab->hra", tile_stack, region_blocks, preferred_element_type=jnp.float32
        )
        spatial = spatial.astype(jnp.bfloat16).reshape(hour_slice, tm_count, own_rows, tile_width)
        blended = temporal(lax.all_to_all(spatial, TM, split_axis=1, concat_axis=0, tiled=True))
        returned = lax.all_to_all(blended, TM, split_axis=0, concat_axis=1, tiled=True)
        return current + returned.reshape(hour_slice, site_count).astype(jnp.float32)

    solution = initial
    residual = right_side - operate(initial)
    direction = residual
    norm_now = one_axis_at_a_time(jnp.sum(residual * residual), REGION_TM)
    for iteration in range(ITERS):
        applied = operate(direction)
        curvature, cross_term, square = (
            one_axis_at_a_time(jnp.sum(direction * applied), REGION_TM),
            one_axis_at_a_time(jnp.sum(residual * applied), REGION_TM),
            one_axis_at_a_time(jnp.sum(applied * applied), REGION_TM),
        )
        step_size = norm_now / curvature
        solution = solution + step_size * direction
        norm_next = norm_now - 2.0 * step_size * cross_term + step_size * step_size * square
        residual = residual - step_size * applied
        if iteration + 1 < ITERS:
            direction = residual + norm_next / norm_now * direction
        norm_now = norm_next
    return (solution, residual)


def solution(mesh):
    split = Mesh(mesh.devices.reshape(4, 8, 8, 2), ("region_0", "region_1", "tm_0", "tm_1"))
    return jax.shard_map(
        local,
        mesh=split,
        in_specs=(
            P(TM, REGION),
            P(TM, REGION),
            P(REGION_TM, None, None, None),
            P(REGION, None),
            P(TM, None),
        ),
        out_specs=(P(TM, REGION), P(TM, REGION)),
        check_vma=False,
    )
```

profile of v0, /device:TPU:1, one launch (start us, length us, event | category | flops | bytes accessed | tf_op | source)
XLA Modules:
  0.0 342.4 jit_solution(12038400127978279072)
XLA Ops:
  7.2 0.7 all-gather.3.cloned.1.call-update
  7.9 10.2 %all_gather.10 = bf16[128,1024]{1,0:T(8,128)(2,1)} all-gather(bf16[64,1024]{1,0:T(8,128)(2,1)} %param.11), channel_id=1, replica_groups=mesh['region_0'=4,'region_1'=8,'tm_0'=8,'tm_1'=2] {'tm_1'}, dimensions={0}, use_global_device_ids=true | all-gather | bytes 393216 | tf_op jit(solution)/shard_map/all_gather | solution.py:28
  18.2 1.1 convert_element_type.81
  19.3 1.9 collective-permute-start
  21.2 7.5 %collective-permute-start.1 = (bf16[64,1024]{1,0:T(8,128)(2,1)S(1)}, bf16[64,1024]{1,0:T(8,128)(2,1)S(1)}, u32[]{:S(2)}, u32[]{:S(2)}) collective-permute-start(bf16[64,1024]{1,0:T(8,128)(2,1)S(1)} %get-tuple-element.27), channel_id=1, source_target_pairs={{16,0},{32,16},{48,32},{64,48},{80,64},{96,80},{112,96},{128,112},... | collective-permute-start | bytes 393224 | tf_op jit(solution)/shard_map/ppermute | solution.py:21
  28.8 0.7 add_select_fusion
  29.8 0.8 collective-permute-done
  30.5 0.9 collective-permute-done.1
  31.6 1.0 gather_fusion
  32.6 27.8 %all-gather.3.cloned.1.call-done = bf16[16,9,128,128]{3,2,1,0:T(8,128)(2,1)} async-done(((bf16[1,9,128,128]{3,2,1,0:T(8,128)(2,1)}), bf16[16,9,128,128]{3,2,1,0:T(8,128)(2,1)}) %all-gather.3.cloned.1.call-update) | async-done | bytes 4718608 | tf_op jit(solution)/shard_map/all_gather | solution.py:53
  60.5 5.0 %fusion.36 = bf16[64,16,1,128]{3,0,2,1:T(8,128)(2,1)} fusion(bf16[16,9,128,128]{3,2,1,0:T(8,128)(2,1)} %all-gather.3.cloned.1.call-done, bf16[16,9,64,128]{3,2,1,0:T(8,128)(2,1)S(1)} %bitcast.174, pred[16,9]{1,0:T(8,128)(4,1)S(1)} %copy.40), kind=kOutput, calls=%fused_computation.30 | convolution fusion | flops 303300608 | bytes 7340176 | tf_op jit(solution)/shard_map/hrkb,rkab->hra/dot_general | solution.py:71
  65.5 5.0 %all-to-all-start = ((bf16[64,16,1,128]{3,0,2,1:T(8,128)(2,1)}), bf16[64,16,1,128]{3,0,2,1:T(8,128)(2,1)S(1)}, u32[]{:S(2)}, u32[]{:S(2)}) async-start(bf16[64,16,1,128]{3,0,2,1:T(8,128)(2,1)} %fusion.36), calls=%async_computation | async-start | bytes 524288 | tf_op jit(solution)/shard_map/all_to_all | solution.py:75
  70.5 31.9 %all-gather.5.cloned.1.call-done = bf16[1024,1024]{1,0:T(8,128)(2,1)} async-done(((bf16[128,1024]{1,0:T(8,128)(2,1)}), bf16[1024,1024]{1,0:T(8,128)(2,1)}) %all-gather.5.cloned.1.call-update) | async-done | bytes 2097168 | tf_op jit(solution)/shard_map/all_gather | solution.py:28
  102.3 2.4 fusion.33
  104.7 0.5 broadcast.101
  105.3 0.8 reduce
  106.3 20.0 %all_to_all.72 = bf16[16,2,4096]{2,1,0:T(2,128)(2,1)S(1)} all-to-all(bf16[16,2,4096]{2,1,0:T(2,128)(2,1)S(1)} %reshape.136), channel_id=1, replica_groups=mesh['region_0'=4,'region_1'=8,'tm_0'=8,'tm_1'=2] {'tm_0','tm_1'}, dimensions={0} | all-to-all | bytes 524288 | tf_op jit(solution)/shard_map/all_to_all | solution.py:76
  127.3 3.3 collective-permute-start.2
  130.6 6.4 %collective-permute-start.3 = (bf16[64,1024]{1,0:T(8,128)(2,1)S(1)}, bf16[64,1024]{1,0:T(8,128)(2,1)S(1)}, u32[]{:S(2)}, u32[]{:S(2)}) collective-permute-start(bf16[64,1024]{1,0:T(8,128)(2,1)S(1)} %get-tuple-element.25), channel_id=1, source_target_pairs={{16,0},{32,16},{48,32},{64,48},{80,64},{96,80},{112,96},{128,112},... | collective-permute-start | bytes 393224 | tf_op jit(solution)/shard_map/ppermute | solution.py:21
  136.9 1.8 collective-permute-done.2
  138.7 1.4 collective-permute-done.3
  140.3 2.5 gather_fusion.1
  142.7 5.1 %fusion.39 = bf16[64,16,1,128]{3,0,2,1:T(8,128)(2,1)S(1)} fusion(bf16[16,9,128,128]{3,2,1,0:T(8,128)(2,1)} %all-gather.3.cloned.1.call-done, bf16[16,9,64,128]{3,2,1,0:T(8,128)(2,1)} %bitcast.176, pred[16,9]{1,0:T(8,128)(4,1)S(1)} %copy.40), kind=kOutput, calls=%fused_computation.31 | convolution fusion | flops 303300608 | bytes 7340176 | tf_op jit(solution)/shard_map/hrkb,rkab->hra/dot_general | solution.py:71
  147.9 14.7 %all_to_all.73 = bf16[64,16,1,128]{3,0,2,1:T(8,128)(2,1)S(1)} all-to-all(bf16[64,16,1,128]{3,0,2,1:T(8,128)(2,1)S(1)} %fusion.39), channel_id=1, replica_groups=mesh['region_0'=4,'region_1'=8,'tm_0'=8,'tm_1'=2] {'tm_0','tm_1'}, dimensions={1} | all-to-all | bytes 524288 | tf_op jit(solution)/shard_map/all_to_all | solution.py:75
  162.6 0.8 fusion.34
  163.4 0.8 reduce.1
  164.5 14.2 %all_to_all.74 = bf16[16,2,4096]{2,1,0:T(2,128)(2,1)S(1)} all-to-all(bf16[16,2,4096]{2,1,0:T(2,128)(2,1)S(1)} %reshape.138), channel_id=1, replica_groups=mesh['region_0'=4,'region_1'=8,'tm_0'=8,'tm_1'=2] {'tm_0','tm_1'}, dimensions={0} | all-to-all | bytes 524288 | tf_op jit(solution)/shard_map/all_to_all | solution.py:76
  179.4 0.9 multiply_reduce_fusion.1
  180.3 7.2 %all-reduce.2 = (f32[]{:T(128)}, f32[]{:T(128)}, f32[]{:T(128)}) all-reduce(f32[]{:T(128)} %get-tuple-element.5, f32[]{:T(128)} %get-tuple-element.4, f32[]{:T(128)} %get-tuple-element.3), channel_id=1, replica_groups=mesh['region_0'=4,'region_1'=8,'tm_0'=8,'tm_1'=2] {'region_0'}, use_global_device_ids=true, to_apply=%region_1.3 | all-reduce | flops 3 | bytes 24 | tf_op jit(solution)/shard_map/psum | solution.py:34
  187.5 16.8 %all-reduce.1 = (f32[]{:T(128)}, f32[]{:T(128)}, f32[]{:T(128)}) all-reduce(f32[]{:T(128)} %get-tuple-element.12, f32[]{:T(128)} %get-tuple-element.13, f32[]{:T(128)} %get-tuple-element.14), channel_id=1, replica_groups=mesh['region_0'=4,'region_1'=8,'tm_0'=8,'tm_1'=2] {'region_1'}, use_global_device_ids=true, to_apply=%region_2.4 | all-reduce | flops 3 | bytes 24 | tf_op jit(solution)/shard_map/psum | solution.py:34
  204.3 11.7 %all-reduce = (f32[]{:T(128)}, f32[]{:T(128)}, f32[]{:T(128)}) all-reduce(f32[]{:T(128)} %get-tuple-element.9, f32[]{:T(128)} %get-tuple-element.10, f32[]{:T(128)} %get-tuple-element.11), channel_id=1, replica_groups=mesh['region_0'=4,'region_1'=8,'tm_0'=8,'tm_1'=2] {'tm_0'}, use_global_device_ids=true, to_apply=%region_3.5 | all-reduce | flops 3 | bytes 24 | tf_op jit(solution)/shard_map/psum | solution.py:34
  216.0 11.5 %all-reduce.3 = (f32[]{:T(128)}, f32[]{:T(128)}, f32[]{:T(128)}) all-reduce(f32[]{:T(128)} %get-tuple-element.6, f32[]{:T(128)} %get-tuple-element.7, f32[]{:T(128)} %get-tuple-element.8), channel_id=1, replica_groups=mesh['region_0'=4,'region_1'=8,'tm_0'=8,'tm_1'=2] {'tm_1'}, use_global_device_ids=true, to_apply=%region_4.6 | all-reduce | flops 3 | bytes 24 | tf_op jit(solution)/shard_map/psum | solution.py:34
  231.4 1.9 collective-permute-start.4
  233.3 6.7 %collective-permute-start.5 = (bf16[64,1024]{1,0:T(8,128)(2,1)S(1)}, bf16[64,1024]{1,0:T(8,128)(2,1)S(1)}, u32[]{:S(2)}, u32[]{:S(2)}) collective-permute-start(bf16[64,1024]{1,0:T(8,128)(2,1)S(1)} %get-tuple-element.23), channel_id=1, source_target_pairs={{16,0},{32,16},{48,32},{64,48},{80,64},{96,80},{112,96},{128,112},... | collective-permute-start | bytes 393224 | tf_op jit(solution)/shard_map/ppermute | solution.py:21
  240.0 1.3 collective-permute-done.4
  241.3 0.9 collective-permute-done.5
  242.4 2.5 gather_fusion.2
  244.9 5.0 %fusion.42 = bf16[64,16,1,128]{3,0,2,1:T(8,128)(2,1)S(1)} fusion(bf16[16,9,128,128]{3,2,1,0:T(8,128)(2,1)} %all-gather.3.cloned.1.call-done, bf16[16,9,64,128]{3,2,1,0:T(8,128)(2,1)} %bitcast.175, pred[16,9]{1,0:T(8,128)(4,1)S(1)} %copy.40), kind=kOutput, calls=%fused_computation.32 | convolution fusion | flops 303300608 | bytes 7340176 | tf_op jit(solution)/shard_map/hrkb,rkab->hra/dot_general | solution.py:71
  249.9 18.4 %all_to_all.75 = bf16[64,16,1,128]{3,0,2,1:T(8,128)(2,1)S(1)} all-to-all(bf16[64,16,1,128]{3,0,2,1:T(8,128)(2,1)S(1)} %fusion.42), channel_id=1, replica_groups=mesh['region_0'=4,'region_1'=8,'tm_0'=8,'tm_1'=2] {'tm_0','tm_1'}, dimensions={1} | all-to-all | bytes 524288 | tf_op jit(solution)/shard_map/all_to_all | solution.py:75
  268.3 0.8 fusion.35
  269.1 0.8 reduce.2
  270.1 14.5 %all_to_all.76 = bf16[16,2,4096]{2,1,0:T(2,128)(2,1)S(1)} all-to-all(bf16[16,2,4096]{2,1,0:T(2,128)(2,1)S(1)} %reshape.140), channel_id=1, replica_groups=mesh['region_0'=4,'region_1'=8,'tm_0'=8,'tm_1'=2] {'tm_0','tm_1'}, dimensions={0} | all-to-all | bytes 524288 | tf_op jit(solution)/shard_map/all_to_all | solution.py:76
  285.3 1.0 multiply_reduce_fusion
  286.4 6.7 %psum.136 = f32[]{:T(128)} all-reduce(f32[]{:T(128)} %multiply_reduce_fusion), channel_id=1, replica_groups=mesh['region_0'=4,'region_1'=8,'tm_0'=8,'tm_1'=2] {'region_0'}, use_global_device_ids=true, to_apply=%region_16.18 | all-reduce | flops 1 | bytes 8 | tf_op jit(solution)/shard_map/psum | solution.py:34
  293.1 17.2 %psum.137 = f32[]{:T(128)} all-reduce(f32[]{:T(128)} %psum.136), channel_id=1, replica_groups=mesh['region_0'=4,'region_1'=8,'tm_0'=8,'tm_1'=2] {'region_1'}, use_global_device_ids=true, to_apply=%region_17.19 | all-reduce | flops 1 | bytes 8 | tf_op jit(solution)/shard_map/psum | solution.py:34
  310.3 11.6 %psum.138 = f32[]{:T(128)} all-reduce(f32[]{:T(128)} %psum.137), channel_id=1, replica_groups=mesh['region_0'=4,'region_1'=8,'tm_0'=8,'tm_1'=2] {'tm_0'}, use_global_device_ids=true, to_apply=%region_18.20 | all-reduce | flops 1 | bytes 8 | tf_op jit(solution)/shard_map/psum | solution.py:34
  321.9 11.5 %psum.139 = f32[]{:T(128)} all-reduce(f32[]{:T(128)} %psum.138), channel_id=1, replica_groups=mesh['region_0'=4,'region_1'=8,'tm_0'=8,'tm_1'=2] {'tm_1'}, use_global_device_ids=true, to_apply=%region_19.21 | all-reduce | flops 1 | bytes 8 | tf_op jit(solution)/shard_map/psum | solution.py:34
  334.1 1.5 multiply_subtract_fusion
  (49 shorter events, 4.0 us)
Async XLA Ops:
  7.2 53.3 %all-gather.3.cloned.1.call-start = ((), (), s32[]{:S(2)}) async-start(), calls=%async_computation.6 | async-start | bytes 5013504 | tf_op jit(solution)/shard_map/all_gather | solution.py:53
  7.9 94.4 %all-gather.5.cloned.1.call-start = ((), (), s32[]{:S(2)}) async-start(), calls=%async_computation.7 | async-start | bytes 2359296 | tf_op jit(solution)/shard_map/all_gather | solution.py:28
  19.3 11.2 %collective-permute-start = (bf16[64,1024]{1,0:T(8,128)(2,1)S(1)}, bf16[64,1024]{1,0:T(8,128)(2,1)S(1)}, u32[]{:S(2)}, u32[]{:S(2)}) collective-permute-start(bf16[64,1024]{1,0:T(8,128)(2,1)S(1)} %get-tuple-element.26), channel_id=1, source_target_pairs={{0,16},{16,32},{32,48},{48,64},{64,80},{80,96},{96,112},{112,128},... | collective-permute-start | bytes 393224 | tf_op jit(solution)/shard_map/ppermute | solution.py:20
  21.2 10.2 %collective-permute-start.1 = (bf16[64,1024]{1,0:T(8,128)(2,1)S(1)}, bf16[64,1024]{1,0:T(8,128)(2,1)S(1)}, u32[]{:S(2)}, u32[]{:S(2)}) collective-permute-start(bf16[64,1024]{1,0:T(8,128)(2,1)S(1)} %get-tuple-element.27), channel_id=1, source_target_pairs={{16,0},{32,16},{48,32},{64,48},{80,64},{96,80},{112,96},{128,112},... | collective-permute-start | bytes 393224 | tf_op jit(solution)/shard_map/ppermute | solution.py:21
  65.5 36.9 %all-to-all-start = ((bf16[64,16,1,128]{3,0,2,1:T(8,128)(2,1)}), bf16[64,16,1,128]{3,0,2,1:T(8,128)(2,1)S(1)}, u32[]{:S(2)}, u32[]{:S(2)}) async-start(bf16[64,16,1,128]{3,0,2,1:T(8,128)(2,1)} %fusion.36), calls=%async_computation | async-start | bytes 524288 | tf_op jit(solution)/shard_map/all_to_all | solution.py:75
  106.2 20.8 %copy-start.3 = (f32[64,2048]{1,0:T(8,128)S(1)}, f32[64,2048]{1,0:T(8,128)}, u32[]{:S(2)}) copy-start(f32[64,2048]{1,0:T(8,128)} %param.8) | copy-start | bytes 1572868
  106.2 20.8 %copy-start.5 = (f32[64,2048]{1,0:T(8,128)S(1)}, f32[64,2048]{1,0:T(8,128)}, u32[]{:S(2)}) copy-start(f32[64,2048]{1,0:T(8,128)} %param.7) | copy-start | bytes 1572868
  127.3 11.4 %collective-permute-start.2 = (bf16[64,1024]{1,0:T(8,128)(2,1)S(1)}, bf16[64,1024]{1,0:T(8,128)(2,1)S(1)}, u32[]{:S(2)}, u32[]{:S(2)}) collective-permute-start(bf16[64,1024]{1,0:T(8,128)(2,1)S(1)} %get-tuple-element.24), channel_id=1, source_target_pairs={{0,16},{16,32},{32,48},{48,64},{64,80},{80,96},{96,112},{112,128},... | collective-permute-start | bytes 393224 | tf_op jit(solution)/shard_map/ppermute | solution.py:20
  130.6 9.5 %collective-permute-start.3 = (bf16[64,1024]{1,0:T(8,128)(2,1)S(1)}, bf16[64,1024]{1,0:T(8,128)(2,1)S(1)}, u32[]{:S(2)}, u32[]{:S(2)}) collective-permute-start(bf16[64,1024]{1,0:T(8,128)(2,1)S(1)} %get-tuple-element.25), channel_id=1, source_target_pairs={{16,0},{32,16},{48,32},{64,48},{80,64},{96,80},{112,96},{128,112},... | collective-permute-start | bytes 393224 | tf_op jit(solution)/shard_map/ppermute | solution.py:21
  142.7 19.8 %copy-start = (bf16[1024,1024]{1,0:T(8,128)(2,1)S(1)}, bf16[1024,1024]{1,0:T(8,128)(2,1)}, u32[]{:S(2)}) copy-start(bf16[1024,1024]{1,0:T(8,128)(2,1)} %all-gather.5.cloned.1.call-done) | copy-start | bytes 6291460
  179.4 62.0 %copy-start.1 = (f32[64,16,1,1,128]{4,1,0,3,2:T(8,128)}, f32[64,16,1,1,128]{4,1,0,3,2:T(8,128)S(1)}, u32[]{:S(2)}) copy-start(f32[64,16,1,1,128]{4,1,0,3,2:T(8,128)S(1)} %copy.53) | copy-start | bytes 1572868
  231.4 9.9 %collective-permute-start.4 = (bf16[64,1024]{1,0:T(8,128)(2,1)S(1)}, bf16[64,1024]{1,0:T(8,128)(2,1)S(1)}, u32[]{:S(2)}, u32[]{:S(2)}) collective-permute-start(bf16[64,1024]{1,0:T(8,128)(2,1)S(1)} %get-tuple-element.22), channel_id=1, source_target_pairs={{0,16},{16,32},{32,48},{48,64},{64,80},{80,96},{96,112},{112,128},... | collective-permute-start | bytes 393224 | tf_op jit(solution)/shard_map/ppermute | solution.py:20
  233.3 8.9 %collective-permute-start.5 = (bf16[64,1024]{1,0:T(8,128)(2,1)S(1)}, bf16[64,1024]{1,0:T(8,128)(2,1)S(1)}, u32[]{:S(2)}, u32[]{:S(2)}) collective-permute-start(bf16[64,1024]{1,0:T(8,128)(2,1)S(1)} %get-tuple-element.23), channel_id=1, source_target_pairs={{16,0},{32,16},{48,32},{64,48},{80,64},{96,80},{112,96},{128,112},... | collective-permute-start | bytes 393224 | tf_op jit(solution)/shard_map/ppermute | solution.py:21
  270.1 15.3 %copy-start.2 = (f32[64,16,1,1,128]{4,1,0,3,2:T(8,128)S(1)}, f32[64,16,1,1,128]{4,1,0,3,2:T(8,128)}, u32[]{:S(2)}) copy-start(f32[64,16,1,1,128]{4,1,0,3,2:T(8,128)} %copy-done.1) | copy-start | bytes 1572868
  284.6 49.4 %copy-start.4 = (f32[64,2048]{1,0:T(8,128)S(1)}, f32[64,2048]{1,0:T(8,128)}, u32[]{:S(2)}) copy-start(f32[64,2048]{1,0:T(8,128)} %param.8) | copy-start | bytes 1572868
Sparse Core Ops, SparseCore 0:
  10.1 50.3 all-gather.2
  62.5 39.7 all-gather.4
where the time goes:
time: 343 us; the launch traced here: 342 us
  blocking collectives  186 us (54%)
  waiting for transfers between devices  67.4 us (20%)
  starting transfers between devices  32.7 us (10%)
  matrix products  19.2 us (6%)
  between operations  18.8 us (5%)
  local copies, waits for them, and re-layouts  9.38 us (3%)
  other arithmetic  8.5 us (2%)
    psum x8, blocking collectives, one_axis_at_a_time(): value = lax.psum(value, axis)  94.3 us
    all_to_all x3, blocking collectives, operate(): lax.all_to_all(blended, TM, split_axis=0, concat_axis=1, tiled=True)  48.7 us
    all_to_all x2, blocking collectives, operate(): lax.all_to_all(spatial, TM, split_axis=1, concat_axis=0, tiled=True)  33.1 us
    all_gather x1, waiting for transfers between devices, gather_axes(): value = lax.all_gather(value, axis, axis=dim, tiled=True)  31.9 us
    all_gather x1, waiting for transfers between devices, local(): region_blocks = lax.all_gather(blocks, TM, axis=0, tiled=True)  27.8 us
    ppermute x3, starting transfers between devices, with_halo(): after = lax.ppermute(initial, axis, down)  20.6 us
    dot_general x3, matrix products, operate(): jnp.einsum('hrkb,rkab->hra', tile_stack, region_blocks, preferred_element...  15.1 us
    all_gather x1, blocking collectives, gather_axes(): value = lax.all_gather(value, axis, axis=dim, tiled=True)  10.2 us
  transfers between devices with their start and end apart: 9, of which 8 were waited for; matrix products, arithmetic and copies ran while one was open for 2% of the time, Pallas kernels for 0%

commit v1 on v0

--- a/solution.py
+++ b/solution.py
@@ -31,7 +31,8 @@
 
 def one_axis_at_a_time(value, axes):
     for axis in axes:
-        value = lax.psum(value, axis)
+        pieces = lax.all_gather(value, axis)
+        value = jnp.sum(pieces, axis=0)
     return value
 
 

time: 343 us -> 374 us (1.090)
  local copies, waits for them, and re-layouts: 9.38 us -> 36.7 us
  blocking collectives: 186 us -> 167 us
  other arithmetic: 8.5 us -> 18.3 us
  waiting for transfers between devices: 67.4 us -> 76.9 us
    psum x8 -> x0, blocking collectives: 94.3 us -> none  [one_axis_at_a_time(): value = lax.psum(value, axis)]
    unnamed x0 -> x8, blocking collectives: none -> 89.3 us
    unnamed x21 -> x57, local copies, waits for them, and re-layouts: 1.53 us -> 28.8 us
    all_to_all x3 -> x2, blocking collectives: 48.7 us -> 34.5 us  [operate(): lax.all_to_all(blended, TM, split_axis=0, concat_axis=1, tiled=True)]
    reduce_sum x0 -> x16, other arithmetic: none -> 9.74 us  [one_axis_at_a_time(): value = jnp.sum(pieces, axis=0)]
    all_to_all x0 -> x1, waiting for transfers between devices: none -> 9.63 us  [operate(): lax.all_to_all(blended, TM, split_axis=0, concat_axis=1, tiled=True)]
  transfers between devices with their start and end apart: 9 -> 10, of which waited for: 8 -> 9; matrix products, arithmetic and copies ran while one was open for 2% -> 3% of each run, Pallas kernels for 0% -> 0%
where the time goes in v1:
time: 374 us; the launch traced here: 373 us
  blocking collectives  167 us (45%)
  waiting for transfers between devices  76.9 us (21%)
  local copies, waits for them, and re-layouts  36.7 us (10%)
  starting transfers between devices  36.4 us (10%)
  matrix products  19.2 us (5%)
  between operations  18.8 us (5%)
  other arithmetic  18.3 us (5%)
    unnamed x8, blocking collectives  89.3 us
    all_to_all x2, blocking collectives, operate(): lax.all_to_all(blended, TM, split_axis=0, concat_axis=1, tiled=True)  34.5 us
    all_to_all x2, blocking collectives, operate(): lax.all_to_all(spatial, TM, split_axis=1, concat_axis=0, tiled=True)  32.8 us
    all_gather x1, waiting for transfers between devices, gather_axes(): value = lax.all_gather(value, axis, axis=dim, tiled=True)  31.9 us
    unnamed x57, local copies, waits for them, and re-layouts  28.8 us
    all_gather x1, waiting for transfers between devices, local(): region_blocks = lax.all_gather(blocks, TM, axis=0, tiled=True)  27.8 us
    ppermute x3, starting transfers between devices, with_halo(): after = lax.ppermute(initial, axis, down)  20.7 us
    dot_general x3, matrix products, operate(): jnp.einsum('hrkb,rkab->hra', tile_stack, region_blocks, preferred_element...  15.1 us
  transfers between devices with their start and end apart: 10, of which 9 were waited for; matrix products, arithmetic and copies ran while one was open for 3% of the time, Pallas kernels for 0%

profile of v1, /device:TPU:1, one launch (start us, length us, event | category | flops | bytes accessed | tf_op | source)
XLA Modules:
  0.0 373.0 jit_solution(5235077481978897174)
XLA Ops:
  7.9 10.2 %all_gather.114 = bf16[128,1024]{1,0:T(8,128)(2,1)} all-gather(bf16[64,1024]{1,0:T(8,128)(2,1)} %param.11), channel_id=1, replica_groups=mesh['region_0'=4,'region_1'=8,'tm_0'=8,'tm_1'=2] {'tm_1'}, dimensions={0}, use_global_device_ids=true | all-gather | bytes 393216 | tf_op jit(solution)/shard_map/all_gather | solution.py:28
  19.3 1.9 collective-permute-start
  21.2 7.5 %collective-permute-start.1 = (bf16[64,1024]{1,0:T(8,128)(2,1)S(1)}, bf16[64,1024]{1,0:T(8,128)(2,1)S(1)}, u32[]{:S(2)}, u32[]{:S(2)}) collective-permute-start(bf16[64,1024]{1,0:T(8,128)(2,1)S(1)} %get-tuple-element.27), channel_id=1, source_target_pairs={{16,0},{32,16},{48,32},{64,48},{80,64},{96,80},{112,96},{128,112},... | collective-permute-start | bytes 393224 | tf_op jit(solution)/shard_map/ppermute | solution.py:21
  32.6 27.8 %all-gather.3.cloned.1.call-done = bf16[16,9,128,128]{3,2,1,0:T(8,128)(2,1)} async-done(((bf16[1,9,128,128]{3,2,1,0:T(8,128)(2,1)}), bf16[16,9,128,128]{3,2,1,0:T(8,128)(2,1)}) %all-gather.3.cloned.1.call-update) | async-done | bytes 4718608 | tf_op jit(solution)/shard_map/all_gather | solution.py:54
  60.5 5.0 %fusion.36 = bf16[64,16,1,128]{3,0,2,1:T(8,128)(2,1)} fusion(bf16[16,9,128,128]{3,2,1,0:T(8,128)(2,1)} %all-gather.3.cloned.1.call-done, bf16[16,9,64,128]{3,2,1,0:T(8,128)(2,1)S(1)} %bitcast.194, pred[16,9]{1,0:T(8,128)(4,1)S(1)} %copy.40), kind=kOutput, calls=%fused_computation.30 | convolution fusion | flops 303300608 | bytes 7340176 | tf_op jit(solution)/shard_map/hrkb,rkab->hra/dot_general | solution.py:72
  65.4 5.0 %all-to-all-start = ((bf16[64,16,1,128]{3,0,2,1:T(8,128)(2,1)}), bf16[64,16,1,128]{3,0,2,1:T(8,128)(2,1)S(1)}, u32[]{:S(2)}, u32[]{:S(2)}) async-start(bf16[64,16,1,128]{3,0,2,1:T(8,128)(2,1)} %fusion.36), calls=%async_computation | async-start | bytes 524288 | tf_op jit(solution)/shard_map/all_to_all | solution.py:76
  70.4 31.9 %all-gather.5.cloned.1.call-done = bf16[1024,1024]{1,0:T(8,128)(2,1)} async-done(((bf16[128,1024]{1,0:T(8,128)(2,1)}), bf16[1024,1024]{1,0:T(8,128)(2,1)}) %all-gather.5.cloned.1.call-update) | async-done | bytes 2097168 | tf_op jit(solution)/shard_map/all_gather | solution.py:28
  102.3 2.4 fusion.33
  106.3 20.0 %all_to_all.72 = bf16[16,2,4096]{2,1,0:T(2,128)(2,1)S(1)} all-to-all(bf16[16,2,4096]{2,1,0:T(2,128)(2,1)S(1)} %reshape.216), channel_id=1, replica_groups=mesh['region_0'=4,'region_1'=8,'tm_0'=8,'tm_1'=2] {'tm_0','tm_1'}, dimensions={0} | all-to-all | bytes 524288 | tf_op jit(solution)/shard_map/all_to_all | solution.py:77
  127.3 3.3 collective-permute-start.2
  130.6 6.4 %collective-permute-start.3 = (bf16[64,1024]{1,0:T(8,128)(2,1)S(1)}, bf16[64,1024]{1,0:T(8,128)(2,1)S(1)}, u32[]{:S(2)}, u32[]{:S(2)}) collective-permute-start(bf16[64,1024]{1,0:T(8,128)(2,1)S(1)} %get-tuple-element.25), channel_id=1, source_target_pairs={{16,0},{32,16},{48,32},{64,48},{80,64},{96,80},{112,96},{128,112},... | collective-permute-start | bytes 393224 | tf_op jit(solution)/shard_map/ppermute | solution.py:21
  136.9 1.8 collective-permute-done.2
  138.7 1.4 collective-permute-done.3
  140.2 2.5 gather_fusion.1
  142.7 5.1 %fusion.39 = bf16[64,16,1,128]{3,0,2,1:T(8,128)(2,1)S(1)} fusion(bf16[16,9,128,128]{3,2,1,0:T(8,128)(2,1)} %all-gather.3.cloned.1.call-done, bf16[16,9,64,128]{3,2,1,0:T(8,128)(2,1)} %bitcast.196, pred[16,9]{1,0:T(8,128)(4,1)S(1)} %copy.40), kind=kOutput, calls=%fused_computation.31 | convolution fusion | flops 303300608 | bytes 7340176 | tf_op jit(solution)/shard_map/hrkb,rkab->hra/dot_general | solution.py:72
  147.9 14.7 %all_to_all.73 = bf16[64,16,1,128]{3,0,2,1:T(8,128)(2,1)S(1)} all-to-all(bf16[64,16,1,128]{3,0,2,1:T(8,128)(2,1)S(1)} %fusion.39), channel_id=1, replica_groups=mesh['region_0'=4,'region_1'=8,'tm_0'=8,'tm_1'=2] {'tm_0','tm_1'}, dimensions={1} | all-to-all | bytes 524288 | tf_op jit(solution)/shard_map/all_to_all | solution.py:76
  165.1 3.4 all-to-all-start.3
  168.6 1.3 dynamic-slice
  169.9 9.6 %all-to-all-done.3 = bf16[16,2,4096]{2,1,0:T(2,128)(2,1)S(1)} async-done(((bf16[16,2,4096]{2,1,0:T(2,128)(2,1)}), bf16[16,2,4096]{2,1,0:T(2,128)(2,1)S(1)}, u32[]{:S(2)}, u32[]{:S(2)}) %all-to-all-start.3) | async-done | bytes 262176 | tf_op jit(solution)/shard_map/all_to_all | solution.py:77
  181.1 1.4 dynamic-update-slice.4
  182.5 1.3 dynamic-update-slice.8
  183.8 1.4 dynamic-update-slice
  185.2 1.3 dynamic-slice.1
  186.5 6.5 %all-reduce.18 = (f32[4]{0:T(128)S(1)}, f32[4]{0:T(128)S(1)}, f32[4]{0:T(128)S(1)}) all-reduce(f32[4]{0:T(128)S(1)} %dynamic-update-slice, f32[4]{0:T(128)S(1)} %dynamic-update-slice.4, f32[4]{0:T(128)S(1)} %dynamic-update-slice.8), channel_id=1, replica_groups=mesh['region_0'=4,'region_1'=8,'tm_0'=8,'tm_1'=2] {'region_0'}, use_global_device_ids=true, to_apply=%add | all-reduce | flops 12 | bytes 96
  194.3 1.3 dynamic-update-slice.9
  200.0 15.9 %all-reduce.17 = (f32[8]{0:T(128)S(1)}, f32[8]{0:T(128)S(1)}, f32[8]{0:T(128)S(1)}) all-reduce(f32[8]{0:T(128)S(1)} %dynamic-update-slice.1, f32[8]{0:T(128)S(1)} %dynamic-update-slice.5, f32[8]{0:T(128)S(1)} %dynamic-update-slice.9), channel_id=1, replica_groups=mesh['region_0'=4,'region_1'=8,'tm_0'=8,'tm_1'=2] {'region_1'}, use_global_device_ids=true, to_apply=%add.1 | all-reduce | flops 24 | bytes 192
  217.1 1.3 dynamic-update-slice.10
  221.5 1.3 dynamic-slice.3
  222.8 10.7 %all-reduce.16 = (f32[8]{0:T(128)S(1)}, f32[8]{0:T(128)S(1)}, f32[8]{0:T(128)S(1)}) all-reduce(f32[8]{0:T(128)S(1)} %dynamic-update-slice.2, f32[8]{0:T(128)S(1)} %dynamic-update-slice.6, f32[8]{0:T(128)S(1)} %dynamic-update-slice.10), channel_id=1, replica_groups=mesh['region_0'=4,'region_1'=8,'tm_0'=8,'tm_1'=2] {'tm_0'}, use_global_device_ids=true, to_apply=%add.2 | all-reduce | flops 24 | bytes 192
  234.7 1.4 dynamic-update-slice.11
  236.1 1.3 dynamic-update-slice.7
  238.1 1.3 dynamic-update-slice.3
  239.4 11.7 %all-reduce.19 = (f32[2]{0:T(128)S(1)}, f32[2]{0:T(128)S(1)}, f32[2]{0:T(128)S(1)}) all-reduce(f32[2]{0:T(128)S(1)} %dynamic-update-slice.3, f32[2]{0:T(128)S(1)} %dynamic-update-slice.7, f32[2]{0:T(128)S(1)} %dynamic-update-slice.11), channel_id=1, replica_groups=mesh['region_0'=4,'region_1'=8,'tm_0'=8,'tm_1'=2] {'tm_1'}, use_global_device_ids=true, to_apply=%add.3 | all-reduce | flops 6 | bytes 48
  256.9 1.9 collective-permute-start.4
  258.8 6.9 %collective-permute-start.5 = (bf16[64,1024]{1,0:T(8,128)(2,1)S(1)}, bf16[64,1024]{1,0:T(8,128)(2,1)S(1)}, u32[]{:S(2)}, u32[]{:S(2)}) collective-permute-start(bf16[64,1024]{1,0:T(8,128)(2,1)S(1)} %get-tuple-element.23), channel_id=1, source_target_pairs={{16,0},{32,16},{48,32},{64,48},{80,64},{96,80},{112,96},{128,112},... | collective-permute-start | bytes 393224 | tf_op jit(solution)/shard_map/ppermute | solution.py:21
  267.9 2.5 gather_fusion.2
  270.4 5.0 %fusion.42 = bf16[64,16,1,128]{3,0,2,1:T(8,128)(2,1)S(1)} fusion(bf16[16,9,128,128]{3,2,1,0:T(8,128)(2,1)} %all-gather.3.cloned.1.call-done, bf16[16,9,64,128]{3,2,1,0:T(8,128)(2,1)} %bitcast.195, pred[16,9]{1,0:T(8,128)(4,1)S(1)} %copy.40), kind=kOutput, calls=%fused_computation.32 | convolution fusion | flops 303300608 | bytes 7340176 | tf_op jit(solution)/shard_map/hrkb,rkab->hra/dot_general | solution.py:72
  275.4 18.1 %all_to_all.74 = bf16[64,16,1,128]{3,0,2,1:T(8,128)(2,1)S(1)} all-to-all(bf16[64,16,1,128]{3,0,2,1:T(8,128)(2,1)S(1)} %fusion.42), channel_id=1, replica_groups=mesh['region_0'=4,'region_1'=8,'tm_0'=8,'tm_1'=2] {'tm_0','tm_1'}, dimensions={1} | all-to-all | bytes 524288 | tf_op jit(solution)/shard_map/all_to_all | solution.py:76
  295.4 14.5 %all_to_all.75 = bf16[16,2,4096]{2,1,0:T(2,128)(2,1)S(1)} all-to-all(bf16[16,2,4096]{2,1,0:T(2,128)(2,1)S(1)} %reshape.220), channel_id=1, replica_groups=mesh['region_0'=4,'region_1'=8,'tm_0'=8,'tm_1'=2] {'tm_0','tm_1'}, dimensions={0} | all-to-all | bytes 524288 | tf_op jit(solution)/shard_map/all_to_all | solution.py:77
  311.6 1.4 dynamic-update-slice.12
  313.0 6.1 %all-reduce.12 = f32[4]{0:T(128)S(1)} all-reduce(f32[4]{0:T(128)S(1)} %dynamic-update-slice.12), channel_id=1, replica_groups=mesh['region_0'=4,'region_1'=8,'tm_0'=8,'tm_1'=2] {'region_0'}, use_global_device_ids=true, to_apply=%add.12 | all-reduce | flops 4 | bytes 32
  319.7 1.4 dynamic-update-slice.13
  321.0 16.5 %all-reduce.13 = f32[8]{0:T(128)S(1)} all-reduce(f32[8]{0:T(128)S(1)} %dynamic-update-slice.13), channel_id=1, replica_groups=mesh['region_0'=4,'region_1'=8,'tm_0'=8,'tm_1'=2] {'region_1'}, use_global_device_ids=true, to_apply=%add.13 | all-reduce | flops 8 | bytes 64
  338.2 1.3 dynamic-update-slice.14
  339.5 11.0 %all-reduce.14 = f32[8]{0:T(128)S(1)} all-reduce(f32[8]{0:T(128)S(1)} %dynamic-update-slice.14), channel_id=1, replica_groups=mesh['region_0'=4,'region_1'=8,'tm_0'=8,'tm_1'=2] {'tm_0'}, use_global_device_ids=true, to_apply=%add.14 | all-reduce | flops 8 | bytes 64
  351.1 1.4 dynamic-update-slice.15
  352.6 10.8 %all-reduce.15 = f32[2]{0:T(128)S(1)} all-reduce(f32[2]{0:T(128)S(1)} %dynamic-update-slice.15), channel_id=1, replica_groups=mesh['region_0'=4,'region_1'=8,'tm_0'=8,'tm_1'=2] {'tm_1'}, use_global_device_ids=true, to_apply=%add.15 | all-reduce | flops 2 | bytes 16
  364.7 1.5 multiply_subtract_fusion
  (102 shorter events, 34.4 us)
Async XLA Ops:
  7.2 53.3 %all-gather.3.cloned.1.call-start = ((), (), s32[]{:S(2)}) async-start(), calls=%async_computation.6 | async-start | bytes 5013504 | tf_op jit(solution)/shard_map/all_gather | solution.py:54
  7.9 94.4 %all-gather.5.cloned.1.call-start = ((), (), s32[]{:S(2)}) async-start(), calls=%async_computation.7 | async-start | bytes 2359296 | tf_op jit(solution)/shard_map/all_gather | solution.py:28
  19.3 11.2 %collective-permute-start = (bf16[64,1024]{1,0:T(8,128)(2,1)S(1)}, bf16[64,1024]{1,0:T(8,128)(2,1)S(1)}, u32[]{:S(2)}, u32[]{:S(2)}) collective-permute-start(bf16[64,1024]{1,0:T(8,128)(2,1)S(1)} %get-tuple-element.26), channel_id=1, source_target_pairs={{0,16},{16,32},{32,48},{48,64},{64,80},{80,96},{96,112},{112,128},... | collective-permute-start | bytes 393224 | tf_op jit(solution)/shard_map/ppermute | solution.py:20
  21.2 10.2 %collective-permute-start.1 = (bf16[64,1024]{1,0:T(8,128)(2,1)S(1)}, bf16[64,1024]{1,0:T(8,128)(2,1)S(1)}, u32[]{:S(2)}, u32[]{:S(2)}) collective-permute-start(bf16[64,1024]{1,0:T(8,128)(2,1)S(1)} %get-tuple-element.27), channel_id=1, source_target_pairs={{16,0},{32,16},{48,32},{64,48},{80,64},{96,80},{112,96},{128,112},... | collective-permute-start | bytes 393224 | tf_op jit(solution)/shard_map/ppermute | solution.py:21
  65.4 36.9 %all-to-all-start = ((bf16[64,16,1,128]{3,0,2,1:T(8,128)(2,1)}), bf16[64,16,1,128]{3,0,2,1:T(8,128)(2,1)S(1)}, u32[]{:S(2)}, u32[]{:S(2)}) async-start(bf16[64,16,1,128]{3,0,2,1:T(8,128)(2,1)} %fusion.36), calls=%async_computation | async-start | bytes 524288 | tf_op jit(solution)/shard_map/all_to_all | solution.py:76
  106.2 20.8 %copy-start.3 = (f32[64,2048]{1,0:T(8,128)S(1)}, f32[64,2048]{1,0:T(8,128)}, u32[]{:S(2)}) copy-start(f32[64,2048]{1,0:T(8,128)} %param.8) | copy-start | bytes 1572868
  106.2 20.8 %copy-start.5 = (f32[64,2048]{1,0:T(8,128)S(1)}, f32[64,2048]{1,0:T(8,128)}, u32[]{:S(2)}) copy-start(f32[64,2048]{1,0:T(8,128)} %param.7) | copy-start | bytes 1572868
  127.3 11.4 %collective-permute-start.2 = (bf16[64,1024]{1,0:T(8,128)(2,1)S(1)}, bf16[64,1024]{1,0:T(8,128)(2,1)S(1)}, u32[]{:S(2)}, u32[]{:S(2)}) collective-permute-start(bf16[64,1024]{1,0:T(8,128)(2,1)S(1)} %get-tuple-element.24), channel_id=1, source_target_pairs={{0,16},{16,32},{32,48},{48,64},{64,80},{80,96},{96,112},{112,128},... | collective-permute-start | bytes 393224 | tf_op jit(solution)/shard_map/ppermute | solution.py:20
  130.6 9.5 %collective-permute-start.3 = (bf16[64,1024]{1,0:T(8,128)(2,1)S(1)}, bf16[64,1024]{1,0:T(8,128)(2,1)S(1)}, u32[]{:S(2)}, u32[]{:S(2)}) collective-permute-start(bf16[64,1024]{1,0:T(8,128)(2,1)S(1)} %get-tuple-element.25), channel_id=1, source_target_pairs={{16,0},{32,16},{48,32},{64,48},{80,64},{96,80},{112,96},{128,112},... | collective-permute-start | bytes 393224 | tf_op jit(solution)/shard_map/ppermute | solution.py:21
  142.7 19.8 %copy-start = (bf16[1024,1024]{1,0:T(8,128)(2,1)S(1)}, bf16[1024,1024]{1,0:T(8,128)(2,1)}, u32[]{:S(2)}) copy-start(bf16[1024,1024]{1,0:T(8,128)(2,1)} %all-gather.5.cloned.1.call-done) | copy-start | bytes 6291460
  165.1 14.4 %all-to-all-start.3 = ((bf16[16,2,4096]{2,1,0:T(2,128)(2,1)}), bf16[16,2,4096]{2,1,0:T(2,128)(2,1)S(1)}, u32[]{:S(2)}, u32[]{:S(2)}) async-start(bf16[16,2,4096]{2,1,0:T(2,128)(2,1)} %reshape.218), calls=%async_computation.3 | async-start | bytes 524288 | tf_op jit(solution)/shard_map/all_to_all | solution.py:77
  180.2 86.6 %copy-start.1 = (f32[64,16,1,1,128]{4,1,0,3,2:T(8,128)}, f32[64,16,1,1,128]{4,1,0,3,2:T(8,128)S(1)}, u32[]{:S(2)}) copy-start(f32[64,16,1,1,128]{4,1,0,3,2:T(8,128)S(1)} %copy.53) | copy-start | bytes 1572868
  256.9 9.9 %collective-permute-start.4 = (bf16[64,1024]{1,0:T(8,128)(2,1)S(1)}, bf16[64,1024]{1,0:T(8,128)(2,1)S(1)}, u32[]{:S(2)}, u32[]{:S(2)}) collective-permute-start(bf16[64,1024]{1,0:T(8,128)(2,1)S(1)} %get-tuple-element.22), channel_id=1, source_target_pairs={{0,16},{16,32},{32,48},{48,64},{64,80},{80,96},{96,112},{112,128},... | collective-permute-start | bytes 393224 | tf_op jit(solution)/shard_map/ppermute | solution.py:20
  258.8 8.9 %collective-permute-start.5 = (bf16[64,1024]{1,0:T(8,128)(2,1)S(1)}, bf16[64,1024]{1,0:T(8,128)(2,1)S(1)}, u32[]{:S(2)}, u32[]{:S(2)}) collective-permute-start(bf16[64,1024]{1,0:T(8,128)(2,1)S(1)} %get-tuple-element.23), channel_id=1, source_target_pairs={{16,0},{32,16},{48,32},{64,48},{80,64},{96,80},{112,96},{128,112},... | collective-permute-start | bytes 393224 | tf_op jit(solution)/shard_map/ppermute | solution.py:21
  295.3 15.3 %copy-start.2 = (f32[64,16,1,1,128]{4,1,0,3,2:T(8,128)S(1)}, f32[64,16,1,1,128]{4,1,0,3,2:T(8,128)}, u32[]{:S(2)}) copy-start(f32[64,16,1,1,128]{4,1,0,3,2:T(8,128)} %copy-done.1) | copy-start | bytes 1572868
  309.9 54.8 %copy-start.4 = (f32[64,2048]{1,0:T(8,128)S(1)}, f32[64,2048]{1,0:T(8,128)}, u32[]{:S(2)}) copy-start(f32[64,2048]{1,0:T(8,128)} %param.8) | copy-start | bytes 1572868
Sparse Core Ops, SparseCore 0:
  10.1 50.3 all-gather.2
  62.5 39.7 all-gather.4
